TPU v7x, 32 devices: a whole 2x2x4 slice. The times are simulated.
32 devices in a mesh: mem: 4 (over y, x), cell: 8 (over z, core).
Axes of the slice: x: 2, y: 2, z: 4, core: 2. Of those that a mesh axis runs over, the one named last changes fastest.
Arguments:
- depth: float32 [64, 131072], P('mem', 'cell'), may hold values from 1 to 3
- discharge: float32 [64, 131072], P('mem', 'cell'), may hold values from -1.5 to 1.5
- gate: int32 [131072], P('cell'), may hold values from 0 to 1, as said below
- pump: int32 [2, 131072], P(None, 'cell'), may hold values 0 or 1
- pump_rate: float32 [131072], P('cell'), may hold values from 1 to 5
- obs_index: int32 [8, 512], P('cell'), may hold values from 0 to 16383, as said below
- obs_value: float32 [8, 512], P('cell'), may hold values from 1 to 3
- obs_error: float32 [8, 512], P('cell'), may hold values from 0.25 to 1.04
Outputs:
- depth_analysis: float32 [64, 131072], P('mem', 'cell')
- discharge_analysis: float32 [64, 131072], P('mem', 'cell')
Inputs may be any that keep to these rules, and one draw needn't show every extreme that they name: The gate on the first face of every slab after the first (cells s * 16384 with s >= 1) is open. `obs_index`: the offsets of one slab are distinct.
All inputs are finite; a program needn't handle non-finite values. No bound on the sum of `pump` on one device may be relied on, other than what follows from the above.
Results may differ from a plain program's by a relative error of at most 0.0003.
Values sent between devices are 32-bit elements; how exact they have to be, the bound alone decides.
A program may use at most 64 MiB of HBM per device.

v0:
```python
import jax
import jax.numpy as jnp
from jax import lax
from jax.sharding import PartitionSpec as P

PER = 512
NS_ITERS = 12
gravity = 9.81
step_dt = 0.06


def padded_2(block, sides, width):
    for axis, dim in sides:
        count = lax.axis_size(axis)
        forward = [(i, i + 1) for i in range(count - 1)]
        backward = [(target, source) for source, target in forward]
        low = lax.ppermute(
            lax.slice_in_dim(block, block.shape[dim] - width, None, axis=dim), axis, forward
        )
        high = lax.ppermute(lax.slice_in_dim(block, 0, width, axis=dim), axis, backward)
        block = jnp.concatenate([low, block, high], axis=dim)
    return block


def face_fluxes(depth_left, flow_left, depth_right, flow_right, faces):
    opened = faces > 0.5
    safe_dl = jnp.where(opened, depth_left, 1.0)
    safe_fl = jnp.where(opened, flow_left, 0.0)
    safe_dr = jnp.where(opened, depth_right, 1.0)
    safe_fr = jnp.where(opened, flow_right, 0.0)
    speed_left = safe_fl / safe_dl
    speed_right = safe_fr / safe_dr
    wave_left = jnp.sqrt(gravity * safe_dl)
    wave_right = jnp.sqrt(gravity * safe_dr)
    slowest = jnp.minimum(jnp.minimum(speed_left - wave_left, speed_right - wave_right), 0.0)
    fastest = jnp.maximum(jnp.maximum(speed_left + wave_left, speed_right + wave_right), 0.0)
    moment_left = safe_fl * speed_left + 0.5 * gravity * safe_dl * safe_dl
    moment_right = safe_fr * speed_right + 0.5 * gravity * safe_dr * safe_dr
    spread = fastest - slowest
    mass = (
        fastest * safe_fl - slowest * safe_fr + slowest * fastest * (safe_dr - safe_dl)
    ) / spread
    moment = (
        fastest * moment_left - slowest * moment_right + slowest * fastest * (safe_fr - safe_fl)
    ) / spread
    mass = jnp.where(opened, mass, 0.0)
    left_side = jnp.where(opened, moment, 0.5 * gravity * depth_left * depth_left)
    right_side = jnp.where(opened, moment, 0.5 * gravity * depth_right * depth_right)
    return (mass, left_side, right_side)


def advance(depth_pad, flow_pad, faces, inflow):
    mass, left_side, right_side = face_fluxes(
        depth_pad[..., :-1], flow_pad[..., :-1], depth_pad[..., 1:], flow_pad[..., 1:], faces
    )
    depth_new = depth_pad[..., 1:-1] - step_dt * (mass[..., 1:] - mass[..., :-1]) + step_dt * inflow
    flow_new = flow_pad[..., 1:-1] - step_dt * (left_side[..., 1:] - right_side[..., :-1])
    return (depth_new, flow_new)


def batch_product(first, second):
    return jnp.einsum("uij,ujk->uik", first, second, precision=lax.Precision.HIGHEST)


def transform_units(grams, cross, factor_rho):
    count = grams.shape[-1]
    identity = jnp.eye(count, dtype=jnp.float32)
    system = identity + factor_rho * factor_rho / (count - 1) * grams
    norm_scale = jnp.sqrt(jnp.sum(system * system, axis=(1, 2)))
    iterate = system / norm_scale[:, None, None]
    inverse = jnp.broadcast_to(identity, system.shape)

    def newton_step(turn, carry):
        current, invroot = carry
        factor = 1.5 * identity - 0.5 * batch_product(invroot, current)
        return (batch_product(current, factor), batch_product(factor, invroot))

    iterate, inverse = lax.fori_loop(0, NS_ITERS, newton_step, (iterate, inverse))
    root_weight = inverse / jnp.sqrt(norm_scale)[:, None, None]
    solved = batch_product(inverse, inverse) / norm_scale[:, None, None]
    mean_weight = (
        factor_rho
        / (count - 1)
        * jnp.einsum("uij,uj->ui", solved, cross, precision=lax.Precision.HIGHEST)
    )
    return factor_rho * (root_weight + mean_weight[:, :, None])


def window_sums(block_grams, block_cross):
    grams = block_grams[:-2] + block_grams[1:-1] + block_grams[2:]
    cross = block_cross[:-2] + block_cross[1:-1] + block_cross[2:]
    return (grams, cross)


def shards(depth, discharge, gate, pump, pump_rate, obs_index, obs_value, obs_error):
    member_rows = depth.shape[0]
    cell_count = depth.shape[1]
    slab_count = lax.axis_size("cell")
    quarter_count = lax.axis_size("mem")
    members = member_rows * quarter_count
    quart_cells = cell_count // quarter_count
    sub_count = quart_cells // PER
    obs_count = obs_index.shape[1]
    total_obs = obs_count * slab_count
    slab_here = lax.axis_index("cell")
    first_slab = slab_here == 0
    last_slab = slab_here == slab_count - 1
    left_open = gate.at[0].set(jnp.where(first_slab, 0, gate[0]))
    right_face = jnp.where(last_slab, 0, 1).astype(jnp.int32).reshape(1)
    faces = jnp.concatenate([left_open, right_face]).astype(jnp.float32)
    depth_now, flow_now = (depth, discharge)
    for step in range(pump.shape[0]):
        padded = padded_2(jnp.stack([depth_now, flow_now]), (("cell", 2),), 1)
        inflow = pump_rate * pump[step].astype(jnp.float32)
        depth_now, flow_now = advance(padded[0], padded[1], faces, inflow)
    offsets = obs_index[0]
    precision_obs = 1.0 / obs_error[0]
    values_obs = obs_value[0]
    value_row = jnp.zeros((cell_count,), jnp.float32).at[offsets].set(values_obs)
    prec_row = jnp.zeros((cell_count,), jnp.float32).at[offsets].set(precision_obs)
    stacked = jnp.concatenate([depth_now, value_row[None, :], prec_row[None, :]], axis=0)
    extended = padded_2(stacked, (("cell", 1),), PER)
    row_total = extended.shape[0]
    seen_local = depth_now[:, offsets]
    seen_all = lax.all_gather(seen_local, "mem", axis=0, tiled=True)
    seen_mean = jnp.mean(seen_all, axis=0)
    scaled_seen = (seen_all - seen_mean[None, :]) * precision_obs[None, :]
    innov_seen = (values_obs - seen_mean) * precision_obs
    total_misfit, total_spread = lax.psum(
        (jnp.sum(innov_seen * innov_seen), jnp.sum(scaled_seen * scaled_seen) / (members - 1)),
        "cell",
    )
    head = extended[:, :cell_count].reshape(row_total, quarter_count, quart_cells)[:, :, :PER]
    core = extended[:, PER : PER + cell_count].reshape(row_total, quarter_count, quart_cells)
    tail = extended[:, 2 * PER :].reshape(row_total, quarter_count, quart_cells)[
        :, :, quart_cells - PER :
    ]
    windows = jnp.concatenate([head, core, tail], axis=2)
    flow_quarters = flow_now.reshape(member_rows, quarter_count, quart_cells)
    moved_depth, moved_flow = (
        lax.all_to_all(windows[:member_rows], "mem", split_axis=1, concat_axis=0, tiled=True),
        lax.all_to_all(flow_quarters, "mem", split_axis=1, concat_axis=0, tiled=True),
    )
    window_depth = moved_depth[:, 0]
    quarter_flow = moved_flow[:, 0]
    obs_window = lax.dynamic_index_in_dim(
        windows[member_rows:], lax.axis_index("mem"), 1, keepdims=False
    )
    window_mean = jnp.mean(window_depth, axis=0)
    scaled = (window_depth - window_mean[None, :]) * obs_window[1][None, :]
    innov = (obs_window[0] - window_mean) * obs_window[1]
    blocks = scaled.reshape(members, sub_count + 2, PER)
    block_grams = jnp.einsum("ibr,jbr->bij", blocks, blocks, precision=lax.Precision.HIGHEST)
    block_cross = jnp.einsum(
        "ibr,br->bi", blocks, innov.reshape(sub_count + 2, PER), precision=lax.Precision.HIGHEST
    )
    grams, cross = window_sums(block_grams, block_cross)
    factor_rho = jnp.sqrt(total_misfit / (total_spread + total_obs))
    mixing = transform_units(grams, cross, factor_rho)
    fields = jnp.stack([window_depth[:, PER : PER + quart_cells], quarter_flow]).reshape(
        2, members, sub_count, PER
    )
    field_mean = jnp.mean(fields, axis=1, keepdims=True)
    analysed = field_mean + jnp.einsum(
        "fipr,pij->fjpr", fields - field_mean, mixing, precision=lax.Precision.HIGHEST
    )
    restored = lax.all_to_all(
        analysed.reshape(2, members, quart_cells), "mem", split_axis=1, concat_axis=2, tiled=True
    )
    return (restored[0], restored[1])


def solution(mesh):
    return jax.shard_map(
        shards,
        mesh=mesh,
        in_specs=(
            P("mem", "cell"),
            P("mem", "cell"),
            P("cell"),
            P(None, "cell"),
            P("cell"),
            P("cell", None),
            P("cell", None),
            P("cell", None),
        ),
        out_specs=(P("mem", "cell"), P("mem", "cell")),
        check_vma=False,
    )
```

profile of v0, /device:TPU:0, one launch (start us, length us, event | category | flops | bytes accessed | tf_op | source)
XLA Modules:
  0.0 180.7 jit_solution(2937933916349297083)
XLA Ops:
  3.7 3.0 %collective-permute-start = (f32[2,16,1]{2,1,0:T(8,128)S(1)}, f32[2,16,1]{2,1,0:T(8,128)S(1)}, u32[]{:S(2)}, u32[]{:S(2)}) collective-permute-start(f32[2,16,1]{2,1,0:T(8,128)S(1)} %get-tuple-element.88), channel_id=1, source_target_pairs={{0,1},{1,2},{2,3},{3,4},{4,5},{5,6},{6,7},{8,9},{9,10},{10,11},{11... | collective-permute-start | bytes 392 | tf_op jit(solution)/shard_map/ppermute | solution.py:17
  7.4 1.5 pad_maximum_fusion
  10.4 2.5 %scatter_custom_fusion.1 = f32[16384]{0:T(1024)S(1)} fusion(s32[512]{0:T(512)S(1)} %bitcast.152, f32[512]{0:T(512)S(1)} %bitcast.146, f32[]{:T(128)} %constant.71.clone.1), kind=kCustom, calls=%fused_computation.138 | custom fusion | bytes 65540 | tf_op jit(solution)/shard_map/scatter | solution.py:120
  12.9 2.5 %scatter_custom_fusion = f32[16384]{0:T(1024)S(1)} fusion(s32[512]{0:T(512)S(1)} %bitcast.153, f32[512]{0:T(512)S(1)} %bitcast.154, f32[]{:T(128)} %constant.71.clone.1), kind=kCustom, calls=%fused_computation.140 | custom fusion | bytes 65540 | tf_op jit(solution)/shard_map/scatter | solution.py:119
  15.4 3.1 %concatenate.34 = f32[2,16,16386]{2,1,0:T(8,128)S(1)} concatenate(f32[2,16,1]{2,1,0:T(8,128)S(1)} %collective-permute-done, f32[2,16,16384]{2,1,0:T(8,128)} %pad_maximum_fusion, f32[2,16,1]{2,1,0:T(8,128)S(1)} %collective-permute-done.1), dimensions={2} | concatenate | bytes 4194816 | tf_op jit(solution)/shard_map/concatenate | solution.py:21
  18.6 2.2 %fusion.12 = (f32[16,16385]{1,0:T(8,128)S(1)}, f32[16,16385]{1,0:T(8,128)S(1)}, f32[16,16385]{1,0:T(8,128)S(1)}, f32[16,16385]{1,0:T(8,128)S(1)}) fusion(f32[16,16386]{1,0:T(8,128)S(1)} %get-tuple-element.82, pred[16385]{0:T(1024)(128)(4,1)S(1)} %fusion.58, f32[16,16386]{1,0:T(8,128)S(1)} %get-tuple-element.81), kind=kLoop, calls=%fused_computation.43 | loop fusion | flops 10748560 | bytes 8405505 | tf_op jit(solution)/shard_map/div | solution.py:43
  20.8 1.4 fusion.26
  23.6 5.2 %collective-permute-start.2 = (f32[2,16,1]{2,1,0:T(8,128)S(1)}, f32[2,16,1]{2,1,0:T(8,128)S(1)}, u32[]{:S(2)}, u32[]{:S(2)}) collective-permute-start(f32[2,16,1]{2,1,0:T(8,128)S(1)} %get-tuple-element.86), channel_id=1, source_target_pairs={{0,1},{1,2},{2,3},{3,4},{4,5},{5,6},{6,7},{8,9},{9,10},{10,11},{11... | collective-permute-start | bytes 392 | tf_op jit(solution)/shard_map/ppermute | solution.py:17
  28.8 1.5 pad_maximum_fusion.1
  30.3 3.1 %concatenate.36 = f32[2,16,16386]{2,1,0:T(8,128)S(1)} concatenate(f32[2,16,1]{2,1,0:T(8,128)S(1)} %collective-permute-done.2, f32[2,16,16384]{2,1,0:T(8,128)} %pad_maximum_fusion.1, f32[2,16,1]{2,1,0:T(8,128)S(1)} %collective-permute-done.3), dimensions={2} | concatenate | bytes 4194816 | tf_op jit(solution)/shard_map/concatenate | solution.py:21
  33.5 2.2 %fusion.19 = (f32[16,16385]{1,0:T(8,128)S(1)}, f32[16,16385]{1,0:T(8,128)S(1)}, f32[16,16385]{1,0:T(8,128)S(1)}, f32[16,16385]{1,0:T(8,128)S(1)}) fusion(f32[16,16386]{1,0:T(8,128)S(1)} %get-tuple-element.80, pred[16385]{0:T(1024)(128)(4,1)S(1)} %fusion.58, f32[16,16386]{1,0:T(8,128)S(1)} %get-tuple-element.79), kind=kLoop, calls=%fused_computation.50 | loop fusion | flops 10748560 | bytes 8405505 | tf_op jit(solution)/shard_map/div | solution.py:43
  36.3 3.6 %collective-permute-start.4 = (f32[18,512]{1,0:T(8,128)S(1)}, f32[18,512]{1,0:T(8,128)S(1)}, u32[]{:S(2)}, u32[]{:S(2)}) collective-permute-start(f32[18,512]{1,0:T(8,128)S(1)} %get-tuple-element.91), channel_id=1, source_target_pairs={{0,1},{1,2},{2,3},{3,4},{4,5},{5,6},{6,7},{8,9},{9,10},{10,11},{11... | collective-permute-start | bytes 110600 | tf_op jit(solution)/shard_map/ppermute | solution.py:17
  42.2 4.6 %copy.124 = f32[16,16384]{0,1:T(8,128)} copy(f32[16,16384]{1,0:T(8,128)S(1)} %fusion.35) | data formatting | bytes 2097152 | tf_op jit(solution)/shard_map/add | solution.py:56
  47.8 4.5 %all-to-all-start.1 = ((f32[16,4,4096]{2,0,1:T(8,128)}), f32[16,4,4096]{2,0,1:T(8,128)}, u32[]{:S(2)}, u32[]{:S(2)}) async-start(f32[16,4,4096]{2,0,1:T(8,128)} %bitcast.97), calls=%async_computation.1 | async-start | bytes 2097152 | tf_op jit(solution)/shard_map/all_to_all | solution.py:142
  52.4 4.4 %gather_fusion = f32[512,16]{1,0:T(8,128)S(1)} fusion(f32[16,16384]{0,1:T(8,128)} %copy.124, s32[1024]{0:T(1024)S(1)} %pad_clamp_fusion), kind=kCustom, calls=%fused_computation | custom fusion | bytes 67584 | tf_op jit(solution)/shard_map/gather | solution.py:124
  56.9 12.8 %all-gather = f32[64,512]{1,0:T(8,128)S(1)} all-gather(f32[16,512]{1,0:T(8,128)S(1)} %copy.125), channel_id=2, replica_groups=mesh['mem'=4,'cell'=8] {'mem'}, dimensions={0}, use_global_device_ids=true | all-gather | bytes 163840 | tf_op jit(solution)/shard_map/all_gather | solution.py:125
  69.8 1.8 %pad_maximum_fusion.6 = (f32[18,16384]{1,0:T(8,128)}, f32[18,16384]{1,0:T(8,128)}) fusion(f32[18,512]{1,0:T(8,128)S(1)} %collective-permute-done.4, f32[1,16384]{1,0:T(1,128)S(1)} %bitcast.133, f32[1,16384]{1,0:T(1,128)S(1)} %bitcast.137, f32[16,16384]{1,0:T(8,128)S(1)} %fusion.35, f32[18,512]{1,0:T(8,128)S(1)} %collective-permute-done.5), kind=kLoop, calls=%fused_computation.31 | loop fusion | flops 1769472 | bytes 3612672 | tf_op jit(solution)/shard_map/concatenate | solution.py:21
  71.6 3.1 %reshape.149 = f32[18,4,4096]{2,1,0:T(4,128)} reshape(f32[18,16384]{1,0:T(8,128)} %get-tuple-element.89) | data formatting | bytes 2359296 | tf_op jit(solution)/shard_map/reshape | solution.py:133
  75.7 1.8 %reshape.150 = f32[18,4,4096]{2,1,0:T(4,128)} reshape(f32[18,16384]{1,0:T(8,128)S(1)} %copy-done) | data formatting | bytes 2359296 | tf_op jit(solution)/shard_map/reshape | solution.py:135
  79.9 3.7 %all-to-all-start = ((f32[16,4,5120]{2,0,1:T(8,128)}), f32[16,4,5120]{2,0,1:T(8,128)S(1)}, u32[]{:S(2)}, u32[]{:S(2)}) async-start(f32[16,4,5120]{2,0,1:T(8,128)} %slice.254), calls=%async_computation | async-start | bytes 2621440 | tf_op jit(solution)/shard_map/all_to_all | solution.py:141
  85.4 16.1 %all-reduce = (f32[]{:T(128)}, f32[]{:T(128)}) all-reduce(f32[]{:T(128)} %get-tuple-element.104, f32[]{:T(128)S(6)} %div.103), channel_id=1, replica_groups=mesh['mem'=4,'cell'=8] {'cell'}, use_global_device_ids=true, to_apply=%region_5.6 | all-reduce | flops 2 | bytes 16 | tf_op jit(solution)/shard_map/psum | solution.py:129
  103.5 2.8 %copy.150 = f32[8,8,8,512]{3,2,1,0:T(8,128)} copy(f32[8,8,8,512]{3,1,2,0:T(8,128)} %bitcast.55) | data formatting | bytes 2097152
  109.3 1.7 squeeze.49
  111.0 1.9 %subtract_multiply_fusion = f32[64,10,512]{2,1,0:T(8,128)S(1)} fusion(f32[64,10,512]{2,1,0:T(8,128)} %squeeze.49, f32[10,512]{1,0:T(8,128)S(1)} %mul.260, f32[10,512]{1,0:T(8,128)S(1)} %div.108), kind=kLoop, calls=%fused_computation.22 | loop fusion | flops 655360 | bytes 2662400 | tf_op jit(solution)/shard_map/mul | solution.py:150
  112.9 2.8 %fusion.43 = f32[10,64,64]{2,1,0:T(8,128)S(1)} fusion(f32[64,10,512]{2,1,0:T(8,128)S(1)} %subtract_multiply_fusion), kind=kOutput, calls=%fused_computation.98 | convolution fusion | flops 251658240 | bytes 1474560 | tf_op jit(solution)/shard_map/ibr,jbr->bij/dot_general | solution.py:153
  115.7 2.0 %fusion.41 = f32[10,1,64]{2,1,0:T(1,128)S(1)} fusion(f32[64,10,512]{2,1,0:T(8,128)S(1)} %subtract_multiply_fusion, f32[10,512,1]{1,0,2:T(8,128)S(1)} %multiply_bitcast_fusion), kind=kOutput, calls=%fused_computation.96 | convolution fusion | flops 3932160 | bytes 1333760 | tf_op jit(solution)/shard_map/ibr,br->bi/dot_general | solution.py:154
  118.1 19.9 %while.14 = (s32[]{:T(128)}, f32[8,64,64]{1,2,0:T(8,128)S(1)}, f32[8,64,64]{2,1,0:T(8,128)S(1)}, s32[]{:T(128)}) while((s32[]{:T(128)}, f32[8,64,64]{1,2,0:T(8,128)S(1)}, f32[8,64,64]{2,1,0:T(8,128)S(1)}, s32[]{:T(128)}) %tuple.56), condition=%wide.region_11.12_spmd.clone, body=%wide.region_10.11_spmd.clone.sunk | while | flops 75571200 | bytes 1736757 | solution.py:78
  138.9 2.1 %bitcast_add_fusion = f32[2,64,8,512]{3,1,0,2:T(8,128)S(1)} fusion(f32[2,64,8,512]{3,1,0,2:T(8,128)S(1)} %copy_dynamic-update-slice_fusion, f32[2,8,512]{2,0,1:T(2,128)S(1)} %broadcast_multiply_fusion, f32[8,64,64]{2,1,0:T(8,128)S(1)} %get-tuple-element.36, f32[8,64]{1,0:T(8,128)S(1)} %broadcast_multiply_fusion.2, f32[8]{0:T(128)S(1)} %get-tuple-element.105, ...), kind=kOutput, calls=%fused_computation.19 | convolution fusion | flops 403800064 | bytes 4360228 | tf_op jit(solution)/shard_map/fipr,pij->fjpr/dot_general | solution.py:164
  142.3 2.8 %reshape.183 = f32[2,64,4096]{2,0,1:T(2,128)} reshape(f32[2,64,8,512]{3,2,0,1:T(8,128)S(1)} %copy.145) | data formatting | bytes 4194304 | tf_op jit(solution)/shard_map/reshape | solution.py:168
  145.1 29.7 %all_to_all.45 = f32[2,64,4096]{2,0,1:T(2,128)S(1)} all-to-all(f32[2,64,4096]{2,0,1:T(2,128)} %reshape.183), channel_id=1, replica_groups=mesh['mem'=4,'cell'=8] {'mem'}, dimensions={1} | all-to-all | bytes 4194304 | tf_op jit(solution)/shard_map/all_to_all | solution.py:167
  176.9 1.6 copy.152
  179.1 1.6 copy.151
  (172 shorter events, 42.7 us)
Async XLA Ops:
  1.5 5.9 %copy-start.2 = (f32[16,16384]{1,0:T(8,128)S(1)}, f32[16,16384]{1,0:T(8,128)}, u32[]{:S(2)}) copy-start(f32[16,16384]{1,0:T(8,128)} %param.12) | copy-start | bytes 3145732
  1.5 5.9 %copy-start.3 = (f32[16,16384]{1,0:T(8,128)S(1)}, f32[16,16384]{1,0:T(8,128)}, u32[]{:S(2)}) copy-start(f32[16,16384]{1,0:T(8,128)} %param.13) | copy-start | bytes 3145732
  2.5 13.0 %collective-permute-start.1 = (f32[2,16,1]{2,1,0:T(8,128)S(1)}, f32[2,16,1]{2,1,0:T(8,128)S(1)}, u32[]{:S(2)}, u32[]{:S(2)}) collective-permute-start(f32[2,16,1]{2,1,0:T(8,128)S(1)} %get-tuple-element.87), channel_id=1, source_target_pairs={{1,0},{2,1},{3,2},{4,3},{5,4},{6,5},{7,6},{9,8},{10,9},{11,10},{12... | collective-permute-start | bytes 392 | tf_op jit(solution)/shard_map/ppermute | solution.py:20
  3.7 11.7 %collective-permute-start = (f32[2,16,1]{2,1,0:T(8,128)S(1)}, f32[2,16,1]{2,1,0:T(8,128)S(1)}, u32[]{:S(2)}, u32[]{:S(2)}) collective-permute-start(f32[2,16,1]{2,1,0:T(8,128)S(1)} %get-tuple-element.88), channel_id=1, source_target_pairs={{0,1},{1,2},{2,3},{3,4},{4,5},{5,6},{6,7},{8,9},{9,10},{10,11},{11... | collective-permute-start | bytes 392 | tf_op jit(solution)/shard_map/ppermute | solution.py:17
  7.4 1.5 copy-start.13
  7.4 1.5 copy-start.14
  7.4 2.8 %copy-start.9 = (s32[2,16384]{1,0:T(2,128)S(1)}, s32[2,16384]{1,0:T(2,128)}, u32[]{:S(2)}) copy-start(s32[2,16384]{1,0:T(2,128)} %param.15) | copy-start | bytes 393220
  7.4 5.4 %copy-start.11 = (f32[16384]{0:T(1024)S(1)}, f32[16384]{0:T(1024)}, u32[]{:S(2)}) copy-start(f32[16384]{0:T(1024)} %param.16) | copy-start | bytes 196612
  7.4 5.5 %copy-start.12 = (f32[1,512]{1,0:T(1,128)S(1)}, f32[1,512]{1,0:T(1,128)}, u32[]{:S(2)}) copy-start(f32[1,512]{1,0:T(1,128)} %param.18) | copy-start | bytes 6148
  22.3 8.0 %collective-permute-start.3 = (f32[2,16,1]{2,1,0:T(8,128)S(1)}, f32[2,16,1]{2,1,0:T(8,128)S(1)}, u32[]{:S(2)}, u32[]{:S(2)}) collective-permute-start(f32[2,16,1]{2,1,0:T(8,128)S(1)} %get-tuple-element.85), channel_id=1, source_target_pairs={{1,0},{2,1},{3,2},{4,3},{5,4},{6,5},{7,6},{9,8},{10,9},{11,10},{12... | collective-permute-start | bytes 392 | tf_op jit(solution)/shard_map/ppermute | solution.py:20
  23.6 6.7 %collective-permute-start.2 = (f32[2,16,1]{2,1,0:T(8,128)S(1)}, f32[2,16,1]{2,1,0:T(8,128)S(1)}, u32[]{:S(2)}, u32[]{:S(2)}) collective-permute-start(f32[2,16,1]{2,1,0:T(8,128)S(1)} %get-tuple-element.86), channel_id=1, source_target_pairs={{0,1},{1,2},{2,3},{3,4},{4,5},{5,6},{6,7},{8,9},{9,10},{10,11},{11... | collective-permute-start | bytes 392 | tf_op jit(solution)/shard_map/ppermute | solution.py:17
  36.3 33.4 %collective-permute-start.4 = (f32[18,512]{1,0:T(8,128)S(1)}, f32[18,512]{1,0:T(8,128)S(1)}, u32[]{:S(2)}, u32[]{:S(2)}) collective-permute-start(f32[18,512]{1,0:T(8,128)S(1)} %get-tuple-element.91), channel_id=1, source_target_pairs={{0,1},{1,2},{2,3},{3,4},{4,5},{5,6},{6,7},{8,9},{9,10},{10,11},{11... | collective-permute-start | bytes 110600 | tf_op jit(solution)/shard_map/ppermute | solution.py:17
  40.0 29.8 %collective-permute-start.5 = (f32[18,512]{1,0:T(8,128)S(1)}, f32[18,512]{1,0:T(8,128)S(1)}, u32[]{:S(2)}, u32[]{:S(2)}) collective-permute-start(f32[18,512]{1,0:T(8,128)S(1)} %get-tuple-element.92), channel_id=1, source_target_pairs={{1,0},{2,1},{3,2},{4,3},{5,4},{6,5},{7,6},{9,8},{10,9},{11,10},{12... | collective-permute-start | bytes 110600 | tf_op jit(solution)/shard_map/ppermute | solution.py:20
  47.8 32.1 %all-to-all-start.1 = ((f32[16,4,4096]{2,0,1:T(8,128)}), f32[16,4,4096]{2,0,1:T(8,128)}, u32[]{:S(2)}, u32[]{:S(2)}) async-start(f32[16,4,4096]{2,0,1:T(8,128)} %bitcast.97), calls=%async_computation.1 | async-start | bytes 2097152 | tf_op jit(solution)/shard_map/all_to_all | solution.py:142
  69.7 1.9 %copy-start.6 = (f32[64,512]{1,0:T(8,128)}, f32[64,512]{1,0:T(8,128)S(1)}, u32[]{:S(2)}) copy-start(f32[64,512]{1,0:T(8,128)S(1)} %all-gather) | copy-start | bytes 393220
  71.6 4.1 %copy-start = (f32[18,16384]{1,0:T(8,128)S(1)}, f32[18,16384]{1,0:T(8,128)}, u32[]{:S(2)}) copy-start(f32[18,16384]{1,0:T(8,128)} %get-tuple-element.90) | copy-start | bytes 3538948
  75.7 2.8 %copy-start.4 = (f32[18,4,512]{2,0,1:T(8,128)}, f32[18,4,512]{2,0,1:T(8,128)S(1)}, u32[]{:S(2)}) copy-start(f32[18,4,512]{2,0,1:T(8,128)S(1)} %copy.119) | copy-start | bytes 442372
  79.9 4.3 %copy-start.7 = (f32[64,512]{1,0:T(8,128)S(1)}, f32[64,512]{1,0:T(8,128)}, u32[]{:S(2)}) copy-start(f32[64,512]{1,0:T(8,128)} %copy-done.6) | copy-start | bytes 393220
  79.9 22.8 %copy-start.5 = (f32[18,4,512]{2,0,1:T(8,128)S(1)}, f32[18,4,512]{2,0,1:T(8,128)}, u32[]{:S(2)}) copy-start(f32[18,4,512]{2,0,1:T(8,128)} %copy-done.4) | copy-start | bytes 442372
  79.9 26.4 %all-to-all-start = ((f32[16,4,5120]{2,0,1:T(8,128)}), f32[16,4,5120]{2,0,1:T(8,128)S(1)}, u32[]{:S(2)}, u32[]{:S(2)}) async-start(f32[16,4,5120]{2,0,1:T(8,128)} %slice.254), calls=%async_computation | async-start | bytes 2621440 | tf_op jit(solution)/shard_map/all_to_all | solution.py:141
  107.2 1.2 copy-start.1
  109.3 1.7 copy-start.10
  115.7 2.0 %copy-start.8 = (f32[64,64]{1,0:T(8,128)S(1)}, f32[64,64]{1,0:T(8,128)}, u32[]{:S(2)}) copy-start(f32[64,64]{1,0:T(8,128)} %fusion.67) | copy-start | bytes 49156
where the time goes:
time: 182 us; the launch traced here: 181 us
  blocking collectives  58.6 us (32%)
  local copies, waits for them, and re-layouts  49.4 us (27%)
  matrix products  26.1 us (14%)
  starting transfers between devices  23.9 us (13%)
  other arithmetic  18 us (10%)
  between operations  3.7 us (2%)
    all_to_all x1, blocking collectives, shards(): lax.all_to_all(analysed.reshape(2, members, quart_cells), 'mem', split_ax...  29.7 us
    dot_general x37, matrix products, batch_product(): jnp.einsum('uij,ujk->uik', first, second, precision=lax.Precision.HIGHEST)  18.8 us
    psum x1, blocking collectives, shards(): lax.psum((jnp.sum(innov_seen * innov_seen), jnp.sum(scaled_seen * scaled_...  16.1 us
    all_gather x1, blocking collectives, shards(): seen_all = lax.all_gather(seen_local, 'mem', axis=0, tiled=True)  12.8 us
    ppermute x3, starting transfers between devices, padded_2(): lax.ppermute(lax.slice_in_dim(block, block.shape[dim] - width, None, axis...  11.9 us
    unnamed x37, local copies, waits for them, and re-layouts  8.82 us
    concatenate x2, local copies, waits for them, and re-layouts, padded_2(): block = jnp.concatenate([low, block, high], axis=dim)  6.12 us
    another operation x5, other arithmetic, shards(): padded = padded_2(jnp.stack([depth_now, flow_now]), (('cell', 2),), 1)  5.41 us
  transfers between devices with their start and end apart: 8, of which 0 were waited for; matrix products, arithmetic and copies ran while one was open for 20% of the time, Pallas kernels for 0%

commit v1 on v0

--- a/solution.py
+++ b/solution.py
@@ -122,7 +122,13 @@
     extended = padded_2(stacked, (("cell", 1),), PER)
     row_total = extended.shape[0]
     seen_local = depth_now[:, offsets]
-    seen_all = lax.all_gather(seen_local, "mem", axis=0, tiled=True)
+    size = lax.axis_size("mem")
+    moving, pieces = (seen_local, [seen_local])
+    for _ in range(size - 1):
+        moving = lax.ppermute(moving, "mem", [(i_2, (i_2 + 1) % size) for i_2 in range(size)])
+        pieces.insert(0, moving)
+    line = jnp.concatenate(pieces, axis=0)
+    seen_all = jnp.roll(line, (lax.axis_index("mem") + 1) * seen_local.shape[0], axis=0)
     seen_mean = jnp.mean(seen_all, axis=0)
     scaled_seen = (seen_all - seen_mean[None, :]) * precision_obs[None, :]
     innov_seen = (values_obs - seen_mean) * precision_obs

time: 182 us -> 200 us (1.099)
  waiting for transfers between devices: 0.02 us -> 22.5 us
  blocking collectives: 58.6 us -> 45.7 us
  local copies, waits for them, and re-layouts: 49.4 us -> 53.6 us
  starting transfers between devices: 23.9 us -> 26.9 us
    ppermute x0 -> x3, waiting for transfers between devices: none -> 21.1 us  [shards(): lax.ppermute(moving, 'mem', [(i_2, (i_2 + 1) % size) for i_2 in range(siz...]
    all_gather x1 -> x0, blocking collectives: 12.8 us -> none  [shards(): seen_all = lax.all_gather(seen_local, 'mem', axis=0, tiled=True)]
    ppermute x0 -> x3, starting transfers between devices: none -> 4.08 us  [shards(): lax.ppermute(moving, 'mem', [(i_2, (i_2 + 1) % size) for i_2 in range(siz...]
    gather x2 -> x1, local copies, waits for them, and re-layouts: 4.51 us -> 5.02 us  [shards(): seen_local = depth_now[:, offsets]]
    unnamed x37 -> x35, local copies, waits for them, and re-layouts: 8.82 us -> 8.56 us
  transfers between devices with their start and end apart: 8 -> 11, of which waited for: 0 -> 4; matrix products, arithmetic and copies ran while one was open for 20% -> 17% of each run, Pallas kernels for 0% -> 0%
where the time goes in v1:
time: 200 us; the launch traced here: 199 us
  local copies, waits for them, and re-layouts  53.6 us (27%)
  blocking collectives  45.7 us (23%)
  starting transfers between devices  26.9 us (13%)
  matrix products  26.1 us (13%)
  waiting for transfers between devices  22.5 us (11%)
  other arithmetic  19.8 us (10%)
  between operations  3.69 us (2%)
    all_to_all x1, blocking collectives, shards(): lax.all_to_all(analysed.reshape(2, members, quart_cells), 'mem', split_ax...  29.7 us
    ppermute x3, waiting for transfers between devices, shards(): lax.ppermute(moving, 'mem', [(i_2, (i_2 + 1) % size) for i_2 in range(siz...  21.1 us
    dot_general x37, matrix products, batch_product(): jnp.einsum('uij,ujk->uik', first, second, precision=lax.Precision.HIGHEST)  18.8 us
    psum x1, blocking collectives, shards(): lax.psum((jnp.sum(innov_seen * innov_seen), jnp.sum(scaled_seen * scaled_...  15.9 us
    ppermute x3, starting transfers between devices, padded_2(): lax.ppermute(lax.slice_in_dim(block, block.shape[dim] - width, None, axis...  11.9 us
    unnamed x35, local copies, waits for them, and re-layouts  8.56 us
    div x2, other arithmetic, face_fluxes(): (fastest * moment_left - slowest * moment_right + slowest * fastest * (sa...  5.46 us
    concatenate x2, local copies, waits for them, and re-layouts, padded_2(): block = jnp.concatenate([low, block, high], axis=dim)  5.46 us
  transfers between devices with their start and end apart: 11, of which 4 were waited for; matrix products, arithmetic and copies ran while one was open for 17% of the time, Pallas kernels for 0%

profile of v1, /device:TPU:0, one launch (start us, length us, event | category | flops | bytes accessed | tf_op | source)
XLA Modules:
  0.0 199.3 jit_solution(14561258437893585830)
XLA Ops:
  3.7 3.0 %collective-permute-start = (f32[2,16,1]{2,1,0:T(8,128)S(1)}, f32[2,16,1]{2,1,0:T(8,128)S(1)}, u32[]{:S(2)}, u32[]{:S(2)}) collective-permute-start(f32[2,16,1]{2,1,0:T(8,128)S(1)} %get-tuple-element.88), channel_id=1, source_target_pairs={{0,1},{1,2},{2,3},{3,4},{4,5},{5,6},{6,7},{8,9},{9,10},{10,11},{11... | collective-permute-start | bytes 392 | tf_op jit(solution)/shard_map/ppermute | solution.py:17
  9.0 2.5 %scatter_custom_fusion.1 = f32[16384]{0:T(1024)S(1)} fusion(s32[512]{0:T(512)S(1)} %bitcast.155, f32[512]{0:T(512)S(1)} %bitcast.149, f32[]{:T(128)} %constant.90.clone.1), kind=kCustom, calls=%fused_computation.139 | custom fusion | bytes 65540 | tf_op jit(solution)/shard_map/scatter | solution.py:120
  11.5 2.6 %scatter_custom_fusion = f32[16384]{0:T(1024)S(1)} fusion(s32[512]{0:T(512)S(1)} %bitcast.156, f32[512]{0:T(512)} %bitcast.157, f32[]{:T(128)} %constant.90.clone.1), kind=kCustom, calls=%fused_computation.141 | custom fusion | bytes 66048 | tf_op jit(solution)/shard_map/scatter | solution.py:119
  15.6 3.1 %concatenate.40 = f32[2,16,16386]{2,1,0:T(8,128)S(1)} concatenate(f32[2,16,1]{2,1,0:T(8,128)S(1)} %collective-permute-done, f32[2,16,16384]{2,1,0:T(8,128)} %pad_maximum_fusion, f32[2,16,1]{2,1,0:T(8,128)S(1)} %collective-permute-done.1), dimensions={2} | concatenate | bytes 4194816 | tf_op jit(solution)/shard_map/concatenate | solution.py:21
  18.8 2.2 %fusion.12 = (f32[16,16385]{1,0:T(8,128)S(1)}, f32[16,16385]{1,0:T(8,128)S(1)}, f32[16,16385]{1,0:T(8,128)S(1)}, f32[16,16385]{1,0:T(8,128)S(1)}) fusion(f32[16,16386]{1,0:T(8,128)S(1)} %get-tuple-element.82, pred[16385]{0:T(1024)(128)(4,1)S(1)} %fusion.58, f32[16,16386]{1,0:T(8,128)S(1)} %get-tuple-element.81), kind=kLoop, calls=%fused_computation.43 | loop fusion | flops 10748560 | bytes 8405505 | tf_op jit(solution)/shard_map/div | solution.py:43
  23.8 5.2 %collective-permute-start.2 = (f32[2,16,1]{2,1,0:T(8,128)S(1)}, f32[2,16,1]{2,1,0:T(8,128)S(1)}, u32[]{:S(2)}, u32[]{:S(2)}) collective-permute-start(f32[2,16,1]{2,1,0:T(8,128)S(1)} %get-tuple-element.86), channel_id=1, source_target_pairs={{0,1},{1,2},{2,3},{3,4},{4,5},{5,6},{6,7},{8,9},{9,10},{10,11},{11... | collective-permute-start | bytes 392 | tf_op jit(solution)/shard_map/ppermute | solution.py:17
  29.8 2.4 %concatenate.42 = f32[2,16,16386]{2,1,0:T(8,128)} concatenate(f32[2,16,1]{2,1,0:T(8,128)S(1)} %collective-permute-done.2, f32[2,16,16384]{2,1,0:T(8,128)S(1)} %pad_maximum_fusion.1, f32[2,16,1]{2,1,0:T(8,128)S(1)} %collective-permute-done.3), dimensions={2} | concatenate | bytes 4194816 | tf_op jit(solution)/shard_map/concatenate | solution.py:21
  32.2 1.7 slice_bitcast_fusion.1
  33.9 3.3 %fusion.19 = (f32[16,16385]{1,0:T(8,128)S(1)}, f32[16,16385]{1,0:T(8,128)S(1)}, f32[16,16385]{1,0:T(8,128)}, f32[16,16385]{1,0:T(8,128)}) fusion(f32[16,16386]{1,0:T(8,128)S(1)} %get-tuple-element.80, pred[16385]{0:T(1024)(128)(4,1)S(1)} %fusion.58, f32[16,16386]{1,0:T(8,128)S(1)} %get-tuple-element.79), kind=kLoop, calls=%fused_computation.50 | loop fusion | flops 10748560 | bytes 8405505 | tf_op jit(solution)/shard_map/div | solution.py:43
  37.8 4.6 %copy.122 = f32[16,16384]{0,1:T(8,128)} copy(f32[16,16384]{1,0:T(8,128)S(1)} %fusion.35) | data formatting | bytes 2097152 | tf_op jit(solution)/shard_map/add | solution.py:56
  42.4 3.7 %collective-permute-start.4 = (f32[18,512]{1,0:T(8,128)S(1)}, f32[18,512]{1,0:T(8,128)S(1)}, u32[]{:S(2)}, u32[]{:S(2)}) collective-permute-start(f32[18,512]{1,0:T(8,128)S(1)} %get-tuple-element.91), channel_id=1, source_target_pairs={{0,1},{1,2},{2,3},{3,4},{4,5},{5,6},{6,7},{8,9},{9,10},{10,11},{11... | collective-permute-start | bytes 110600 | tf_op jit(solution)/shard_map/ppermute | solution.py:17
  47.4 5.0 %gather_fusion = f32[512,16]{1,0:T(8,128)} fusion(f32[16,16384]{0,1:T(8,128)} %copy.122, s32[1024]{0:T(1024)S(1)} %pad_clamp_fusion), kind=kCustom, calls=%fused_computation | custom fusion | bytes 67584 | tf_op jit(solution)/shard_map/gather | solution.py:124
  53.9 2.4 %fusion.31 = f32[16,16384]{1,0:T(8,128)S(1)} fusion(f32[16,16385]{1,0:T(8,128)S(1)} %get-tuple-element.75, f32[16,16385]{1,0:T(8,128)} %get-tuple-element.94, f32[16,16385]{1,0:T(8,128)} %get-tuple-element.93, f32[16,16386]{1,0:T(8,128)S(1)} %get-tuple-element.80, pred[16384]{0:T(1024)(128)(4,1)S(1)} %get-tuple-element.102, ...), kind=kLoop, calls=%fused_computation.80 | loop fusion | flops 2359296 | bytes 6324224 | tf_op jit(solution)/shard_map/sub | solution.py:57
  57.4 3.5 %all-to-all-start.1 = ((f32[16,4,4096]{2,0,1:T(8,128)}), f32[16,4,4096]{2,0,1:T(8,128)S(1)}, u32[]{:S(2)}, u32[]{:S(2)}) async-start(f32[16,4,4096]{2,0,1:T(8,128)} %bitcast.97), calls=%async_computation.1 | async-start | bytes 2097152 | tf_op jit(solution)/shard_map/all_to_all | solution.py:148
  61.0 2.0 %collective-permute-start.7 = (f32[16,512]{0,1:T(8,128)}, f32[16,512]{0,1:T(8,128)}, u32[]{:S(2)}, u32[]{:S(2)}) collective-permute-start(f32[16,512]{0,1:T(8,128)} %collective-permute-done.6), channel_id=1, source_target_pairs={{0,8},{8,16},{16,24},{24,0},{1,9},{9,17},{17,25},{25,1},{2,10},{10... | collective-permute-start | bytes 98312 | tf_op jit(solution)/shard_map/ppermute | solution.py:128
  63.0 1.8 pad_maximum_fusion.6
  64.9 3.0 %reshape.149 = f32[18,4,4096]{2,1,0:T(4,128)} reshape(f32[18,16384]{1,0:T(8,128)} %get-tuple-element.89) | data formatting | bytes 2359296 | tf_op jit(solution)/shard_map/reshape | solution.py:139
  68.9 3.0 %reshape.150 = f32[18,4,4096]{2,1,0:T(4,128)} reshape(f32[18,16384]{1,0:T(8,128)} %get-tuple-element.90) | data formatting | bytes 2359296 | tf_op jit(solution)/shard_map/reshape | solution.py:141
  75.9 3.5 %all-to-all-start = ((f32[16,4,5120]{2,0,1:T(8,128)}), f32[16,4,5120]{2,0,1:T(8,128)S(1)}, u32[]{:S(2)}, u32[]{:S(2)}) async-start(f32[16,4,5120]{2,0,1:T(8,128)} %slice.254), calls=%async_computation | async-start | bytes 2621440 | tf_op jit(solution)/shard_map/all_to_all | solution.py:147
  82.2 19.6 %collective-permute-done.8 = f32[16,512]{0,1:T(8,128)S(1)} collective-permute-done((f32[16,512]{0,1:T(8,128)}, f32[16,512]{0,1:T(8,128)S(1)}, u32[]{:S(2)}, u32[]{:S(2)}) %collective-permute-start.8) | collective-permute-done | bytes 32800 | tf_op jit(solution)/shard_map/ppermute | solution.py:128
  101.9 1.9 concatenate.51
  106.1 15.9 %all-reduce = (f32[]{:T(128)}, f32[]{:T(128)}) all-reduce(f32[]{:T(128)} %get-tuple-element.104, f32[]{:T(128)S(6)} %div.103), channel_id=1, replica_groups=mesh['mem'=4,'cell'=8] {'cell'}, use_global_device_ids=true, to_apply=%region_5.6 | all-reduce | flops 2 | bytes 16 | tf_op jit(solution)/shard_map/psum | solution.py:135
  127.9 1.7 squeeze.49
  129.6 1.9 subtract_multiply_fusion
  131.4 2.8 %fusion.43 = f32[10,64,64]{2,1,0:T(8,128)S(1)} fusion(f32[64,10,512]{2,1,0:T(8,128)S(1)} %subtract_multiply_fusion), kind=kOutput, calls=%fused_computation.98 | convolution fusion | flops 251658240 | bytes 1474560 | tf_op jit(solution)/shard_map/ibr,jbr->bij/dot_general | solution.py:159
  134.2 2.0 fusion.41
  136.7 19.9 %while.14 = (s32[]{:T(128)}, f32[8,64,64]{1,2,0:T(8,128)S(1)}, f32[8,64,64]{2,1,0:T(8,128)S(1)}, s32[]{:T(128)}) while((s32[]{:T(128)}, f32[8,64,64]{1,2,0:T(8,128)S(1)}, f32[8,64,64]{2,1,0:T(8,128)S(1)}, s32[]{:T(128)}) %tuple.56), condition=%wide.region_11.12_spmd.clone, body=%wide.region_10.11_spmd.clone.sunk | while | flops 75571200 | bytes 1736757 | solution.py:78
  157.5 2.1 %bitcast_add_fusion = f32[2,64,8,512]{3,1,0,2:T(8,128)S(1)} fusion(f32[2,64,8,512]{3,1,0,2:T(8,128)S(1)} %copy_dynamic-update-slice_fusion, f32[2,8,512]{2,0,1:T(2,128)S(1)} %broadcast_multiply_fusion, f32[8,64,64]{2,1,0:T(8,128)S(1)} %get-tuple-element.36, f32[8,64]{1,0:T(8,128)S(1)} %broadcast_multiply_fusion.2, f32[8]{0:T(128)S(1)} %get-tuple-element.105, ...), kind=kOutput, calls=%fused_computation.19 | convolution fusion | flops 403800064 | bytes 4360228 | tf_op jit(solution)/shard_map/fipr,pij->fjpr/dot_general | solution.py:170
  160.8 2.8 %reshape.182 = f32[2,64,4096]{2,0,1:T(2,128)} reshape(f32[2,64,8,512]{3,2,0,1:T(8,128)S(1)} %copy.142) | data formatting | bytes 4194304 | tf_op jit(solution)/shard_map/reshape | solution.py:174
  163.6 29.7 %all_to_all.45 = f32[2,64,4096]{2,0,1:T(2,128)S(1)} all-to-all(f32[2,64,4096]{2,0,1:T(2,128)} %reshape.182), channel_id=1, replica_groups=mesh['mem'=4,'cell'=8] {'mem'}, dimensions={1} | all-to-all | bytes 4194304 | tf_op jit(solution)/shard_map/all_to_all | solution.py:173
  195.4 1.6 copy.149
  197.7 1.6 copy.148
  (175 shorter events, 52.5 us)
Async XLA Ops:
  1.5 5.9 %copy-start.3 = (f32[16,16384]{1,0:T(8,128)S(1)}, f32[16,16384]{1,0:T(8,128)}, u32[]{:S(2)}) copy-start(f32[16,16384]{1,0:T(8,128)} %param.12) | copy-start | bytes 3145732
  1.5 5.9 %copy-start.4 = (f32[16,16384]{1,0:T(8,128)S(1)}, f32[16,16384]{1,0:T(8,128)}, u32[]{:S(2)}) copy-start(f32[16,16384]{1,0:T(8,128)} %param.13) | copy-start | bytes 3145732
  2.5 13.1 %collective-permute-start.1 = (f32[2,16,1]{2,1,0:T(8,128)S(1)}, f32[2,16,1]{2,1,0:T(8,128)S(1)}, u32[]{:S(2)}, u32[]{:S(2)}) collective-permute-start(f32[2,16,1]{2,1,0:T(8,128)S(1)} %get-tuple-element.87), channel_id=1, source_target_pairs={{1,0},{2,1},{3,2},{4,3},{5,4},{6,5},{7,6},{9,8},{10,9},{11,10},{12... | collective-permute-start | bytes 392 | tf_op jit(solution)/shard_map/ppermute | solution.py:20
  3.7 11.8 %collective-permute-start = (f32[2,16,1]{2,1,0:T(8,128)S(1)}, f32[2,16,1]{2,1,0:T(8,128)S(1)}, u32[]{:S(2)}, u32[]{:S(2)}) collective-permute-start(f32[2,16,1]{2,1,0:T(8,128)S(1)} %get-tuple-element.88), channel_id=1, source_target_pairs={{0,1},{1,2},{2,3},{3,4},{4,5},{5,6},{6,7},{8,9},{9,10},{10,11},{11... | collective-permute-start | bytes 392 | tf_op jit(solution)/shard_map/ppermute | solution.py:17
  7.4 1.5 copy-start.12
  7.4 1.5 copy-start.13
  7.4 8.0 %copy-start.6 = (s32[2,16384]{1,0:T(2,128)S(1)}, s32[2,16384]{1,0:T(2,128)}, u32[]{:S(2)}) copy-start(s32[2,16384]{1,0:T(2,128)} %param.15) | copy-start | bytes 393220
  7.4 8.1 %copy-start.8 = (f32[16384]{0:T(1024)S(1)}, f32[16384]{0:T(1024)}, u32[]{:S(2)}) copy-start(f32[16384]{0:T(1024)} %param.16) | copy-start | bytes 196612
  8.9 6.6 %copy-start.9 = (f32[1,512]{1,0:T(1,128)}, f32[1,512]{1,0:T(1,128)S(1)}, u32[]{:S(2)}) copy-start(f32[1,512]{1,0:T(1,128)S(1)} %broadcast_divide_fusion.1) | copy-start | bytes 6148
  22.5 6.7 %collective-permute-start.3 = (f32[2,16,1]{2,1,0:T(8,128)S(1)}, f32[2,16,1]{2,1,0:T(8,128)S(1)}, u32[]{:S(2)}, u32[]{:S(2)}) collective-permute-start(f32[2,16,1]{2,1,0:T(8,128)S(1)} %get-tuple-element.85), channel_id=1, source_target_pairs={{1,0},{2,1},{3,2},{4,3},{5,4},{6,5},{7,6},{9,8},{10,9},{11,10},{12... | collective-permute-start | bytes 392 | tf_op jit(solution)/shard_map/ppermute | solution.py:20
  23.8 6.0 %collective-permute-start.2 = (f32[2,16,1]{2,1,0:T(8,128)S(1)}, f32[2,16,1]{2,1,0:T(8,128)S(1)}, u32[]{:S(2)}, u32[]{:S(2)}) collective-permute-start(f32[2,16,1]{2,1,0:T(8,128)S(1)} %get-tuple-element.86), channel_id=1, source_target_pairs={{0,1},{1,2},{2,3},{3,4},{4,5},{5,6},{6,7},{8,9},{9,10},{10,11},{11... | collective-permute-start | bytes 392 | tf_op jit(solution)/shard_map/ppermute | solution.py:17
  42.4 20.6 %collective-permute-start.4 = (f32[18,512]{1,0:T(8,128)S(1)}, f32[18,512]{1,0:T(8,128)S(1)}, u32[]{:S(2)}, u32[]{:S(2)}) collective-permute-start(f32[18,512]{1,0:T(8,128)S(1)} %get-tuple-element.91), channel_id=1, source_target_pairs={{0,1},{1,2},{2,3},{3,4},{4,5},{5,6},{6,7},{8,9},{9,10},{10,11},{11... | collective-permute-start | bytes 110600 | tf_op jit(solution)/shard_map/ppermute | solution.py:17
  46.1 16.9 %collective-permute-start.5 = (f32[18,512]{1,0:T(8,128)S(1)}, f32[18,512]{1,0:T(8,128)S(1)}, u32[]{:S(2)}, u32[]{:S(2)}) collective-permute-start(f32[18,512]{1,0:T(8,128)S(1)} %get-tuple-element.92), channel_id=1, source_target_pairs={{1,0},{2,1},{3,2},{4,3},{5,4},{6,5},{7,6},{9,8},{10,9},{11,10},{12... | collective-permute-start | bytes 110600 | tf_op jit(solution)/shard_map/ppermute | solution.py:20
  52.4 8.6 %collective-permute-start.6 = (f32[16,512]{0,1:T(8,128)}, f32[16,512]{0,1:T(8,128)}, u32[]{:S(2)}, u32[]{:S(2)}) collective-permute-start(f32[16,512]{0,1:T(8,128)} %bitcast.141), channel_id=1, source_target_pairs={{0,8},{8,16},{16,24},{24,0},{1,9},{9,17},{17,25},{25,1},{2,10},{10... | collective-permute-start | bytes 98312 | tf_op jit(solution)/shard_map/ppermute | solution.py:128
  57.4 17.5 %all-to-all-start.1 = ((f32[16,4,4096]{2,0,1:T(8,128)}), f32[16,4,4096]{2,0,1:T(8,128)S(1)}, u32[]{:S(2)}, u32[]{:S(2)}) async-start(f32[16,4,4096]{2,0,1:T(8,128)} %bitcast.97), calls=%async_computation.1 | async-start | bytes 2097152 | tf_op jit(solution)/shard_map/all_to_all | solution.py:148
  61.0 19.9 %collective-permute-start.7 = (f32[16,512]{0,1:T(8,128)}, f32[16,512]{0,1:T(8,128)}, u32[]{:S(2)}, u32[]{:S(2)}) collective-permute-start(f32[16,512]{0,1:T(8,128)} %collective-permute-done.6), channel_id=1, source_target_pairs={{0,8},{8,16},{16,24},{24,0},{1,9},{9,17},{17,25},{25,1},{2,10},{10... | collective-permute-start | bytes 98312 | tf_op jit(solution)/shard_map/ppermute | solution.py:128
  74.9 1.0 copy-start
  75.9 49.0 %all-to-all-start = ((f32[16,4,5120]{2,0,1:T(8,128)}), f32[16,4,5120]{2,0,1:T(8,128)S(1)}, u32[]{:S(2)}, u32[]{:S(2)}) async-start(f32[16,4,5120]{2,0,1:T(8,128)} %slice.254), calls=%async_computation | async-start | bytes 2621440 | tf_op jit(solution)/shard_map/all_to_all | solution.py:147
  80.9 20.9 %collective-permute-start.8 = (f32[16,512]{0,1:T(8,128)}, f32[16,512]{0,1:T(8,128)S(1)}, u32[]{:S(2)}, u32[]{:S(2)}) collective-permute-start(f32[16,512]{0,1:T(8,128)} %collective-permute-done.7), channel_id=1, source_target_pairs={{0,8},{8,16},{16,24},{24,0},{1,9},{9,17},{17,25},{25,1},{2,10},{10... | collective-permute-start | bytes 98312 | tf_op jit(solution)/shard_map/ppermute | solution.py:128
  82.2 21.9 %copy-start.10 = (f32[1,512]{1,0:T(1,128)S(1)}, f32[1,512]{1,0:T(1,128)}, u32[]{:S(2)}) copy-start(f32[1,512]{1,0:T(1,128)} %copy-done.9) | copy-start | bytes 6148
  82.2 21.9 %copy-start.11 = (f32[1,512]{1,0:T(1,128)S(1)}, f32[1,512]{1,0:T(1,128)}, u32[]{:S(2)}) copy-start(f32[1,512]{1,0:T(1,128)} %param.18) | copy-start | bytes 6148
  82.2 41.1 %copy-start.1 = (f32[16,4,4096]{2,0,1:T(8,128)S(1)}, f32[16,4,4096]{2,0,1:T(8,128)}, u32[]{:S(2)}) copy-start(f32[16,4,4096]{2,0,1:T(8,128)} %copy-done) | copy-start | bytes 3145732
  125.7 1.2 copy-start.2
  127.9 1.7 copy-start.7
  134.2 2.0 copy-start.5
